TPU v7x, 256 devices: a whole 4x4x8 slice. The times are simulated.
256 devices in a mesh: tm: 32 (over y, z), space: 8 (over x, core).
Axes of the slice: x: 4, y: 4, z: 8, core: 2. Of those that a mesh axis runs over, the one named last changes fastest.
Arguments:
- inverse_factor: bfloat16 [2, 32, 4096, 4096], P(None, 'tm', 'space'), may hold values from -1.5 to 1.5, as said below
- tile_mask: int32 [32, 32], replicated, may hold values 0 or 1
- carry_rate: float32 [32, 4096, 2], P('tm', 'space'), may hold values from 0 to 1
- right_side: float32 [32, 4096, 2, 128], P('tm', 'space'), may hold values from -1.5 to 1.5
- arrow_rows: bfloat16 [32, 4096, 2, 512], P('tm', 'space'), may hold values from -0.0625 to 0.0625
- fixed_rhs: float32 [2, 512, 128], P(None, ('tm', 'space')), may hold values from -6 to 6
- tip_factor: bfloat16 [2, 512, 512], replicated, may hold values from -1 to 1, as said below
Outputs:
- solution: float32 [32, 4096, 2, 128], P('tm', 'space')
- fixed_solution: float32 [2, 512, 128], P(None, ('tm', 'space'))
Inputs may be any that keep to these rules, and one draw needn't show every extreme that they name: `tile_mask`: 1 marks a tile that may be nonzero. `inverse_factor`: only entries on or below the diagonal are read. `tip_factor`: only entries on or below the diagonal are read.
All inputs are finite; a program needn't handle non-finite values.
Results may differ from a plain program's by a relative error of at most 0.022.
Values may be sent and summed in bfloat16 or wider, within the bound.
No kernel may reach another device: no remote copies, remote signals or barrier semaphores. Data moves between devices by JAX's collectives and lax.ppermute only.
A program may use at most 320 MiB of HBM per device.

v0:
```python
import jax
import jax.numpy as jnp
from jax import lax
from jax.sharding import PartitionSpec as P

TILE = 128


def carried_in(shard, axis, join, neutral, backward):
    count = lax.axis_size(axis)
    place = lax.axis_index(axis)
    ahead = count - 1 - place if backward else place
    gathered = jax.tree.map(
        lambda a, kind: lax.all_gather(a.astype(kind), axis), shard, (jnp.bfloat16, jnp.bfloat16)
    )
    state = jax.tree.map(lambda a, e: jnp.zeros_like(a) + jnp.asarray(e, a.dtype), shard, neutral)

    def one(turn, state):
        source = count - 1 - turn if backward else turn
        return join(
            state,
            jax.tree.map(
                lambda a, own: lax.dynamic_index_in_dim(a, source, 0, False).astype(own.dtype),
                gathered,
                shard,
            ),
        )

    return lax.fori_loop(0, ahead, one, state)


def combine(earlier, latter):
    rate_new = latter[0] * earlier[0]
    rest = tuple(
        (value_l + latter[0] * value_e for value_l, value_e in zip(latter[1:], earlier[1:]))
    )
    return (rate_new,) + rest


def tile_keep(tile_table, row_start, row_total, col_total):
    tile_count = tile_table.shape[0]
    tile_ids = jnp.arange(tile_count, dtype=jnp.int32)
    row_index = row_start + jnp.arange(row_total, dtype=jnp.int32)
    col_index = jnp.arange(col_total, dtype=jnp.int32)
    row_onehot = (row_index[:, None] // TILE == tile_ids[None, :]).astype(jnp.float32)
    col_onehot = (col_index[:, None] // TILE == tile_ids[None, :]).astype(jnp.float32)
    marked = jnp.dot(jnp.dot(row_onehot, tile_table.astype(jnp.float32)), col_onehot.T)
    return (marked > 0.5) & (row_index[:, None] >= col_index[None, :])


def on_device(inverse_factor, tile_mask, carry_rate, right_side, arrow_rows, fixed_rhs, tip_factor):
    row_count = right_side.shape[1]
    node_total = inverse_factor.shape[3]
    row_start = lax.axis_index("space") * row_count
    tile_table = jnp.maximum(tile_mask, jnp.eye(tile_mask.shape[0], dtype=jnp.int32))
    weights = inverse_factor[:, 0]
    bf_zero = jnp.zeros((), jnp.bfloat16)
    rate_col = carry_rate[0][:, :, None]
    source = right_side[0]
    unit_rate = jnp.ones_like(rate_col)
    earlier_sum = carried_in(
        (rate_col, source), "tm", combine, (unit_rate, jnp.zeros_like(source)), False
    )
    forward = source + rate_col * earlier_sum[1]
    forward_b = forward.astype(jnp.bfloat16)
    row_keep = tile_keep(tile_table, row_start, row_count, node_total)
    masked_rows = jnp.where(row_keep[None], weights, bf_zero)
    block = masked_rows
    inner_rows = jnp.einsum(
        "hrn,nhk->rhk",
        block,
        lax.all_gather(forward_b, "space", axis=0, tiled=True),
        preferred_element_type=jnp.float32,
    ).astype(jnp.bfloat16)
    block = masked_rows
    scaled = lax.psum_scatter(
        jnp.einsum("hrn,rhk->nhk", block, inner_rows, preferred_element_type=jnp.float32).astype(
            jnp.bfloat16
        ),
        "space",
        scatter_dimension=0,
        tiled=True,
    ).astype(jnp.float32)
    arrow_part = arrow_rows[0]
    coupling = jnp.einsum("rhf,rhk->hfk", arrow_part, forward_b, preferred_element_type=jnp.float32)
    share_rows = fixed_rhs.shape[1]
    share_start = lax.axis_index(("tm", "space")) * share_rows
    contrib = -coupling
    own_part = lax.dynamic_slice_in_dim(contrib, share_start, share_rows, 1) + fixed_rhs
    contrib = lax.dynamic_update_slice_in_dim(contrib, own_part, share_start, 1)
    fixed_forward = lax.psum(contrib, ("tm", "space")).astype(jnp.bfloat16)
    fixed_total = tip_factor.shape[1]
    fixed_index = jnp.arange(fixed_total, dtype=jnp.int32)
    lower_tri = fixed_index[:, None] >= fixed_index[None, :]
    tip_lower = jnp.where(lower_tri[None], tip_factor, bf_zero)
    tip_inner = jnp.einsum(
        "hij,hjk->hik", tip_lower, fixed_forward, preferred_element_type=jnp.float32
    ).astype(jnp.bfloat16)
    fixed_solution = jnp.einsum(
        "hij,hik->hjk", tip_lower, tip_inner, preferred_element_type=jnp.float32
    )
    fixed_own = lax.dynamic_slice_in_dim(fixed_solution, share_start, share_rows, 1)
    fixed_b = fixed_solution.astype(jnp.bfloat16)
    carried = scaled - jnp.einsum(
        "rhf,hfk->rhk", arrow_part, fixed_b, preferred_element_type=jnp.float32
    )
    following = carried_in(
        (rate_col, rate_col * carried), "tm", combine, (unit_rate, jnp.zeros_like(carried)), True
    )
    solution = carried + following[1]
    return (solution[None], fixed_own)


def solution(mesh):
    placed = (
        P(None, "tm", "space", None),
        P(),
        P("tm", "space", None),
        P("tm", "space", None, None),
        P("tm", "space", None, None),
        P(None, ("tm", "space"), None),
        P(),
    )
    return jax.shard_map(
        on_device,
        mesh=mesh,
        in_specs=placed,
        out_specs=(P("tm", "space", None, None), P(None, ("tm", "space"), None)),
        check_vma=False,
    )
```

profile of v0, /device:TPU:2, one launch (start us, length us, event | category | flops | bytes accessed | tf_op | source)
XLA Modules:
  0.0 596.0 jit_solution(12626880782622736189)
XLA Ops:
  7.2 1.9 copy.62
  9.2 1.2 copy.34
  11.1 52.1 %all-gather = bf16[32,512,2]{1,2,0:T(2,128)(2,1)S(1)} all-gather(bf16[1,512,2]{1,2,0:T(2,128)(2,1)S(1)} %convert_element_type.103), channel_id=2, replica_groups=mesh['tm'=32,'space'=8] {'tm'}, dimensions={0}, use_global_device_ids=true | all-gather | bytes 67584 | tf_op jit(solution)/shard_map/all_gather | solution.py:14
  63.2 3.3 copy.37
  66.6 46.1 %all-gather.6.cloned.1.call-done = bf16[32,512,2,128]{3,1,2,0:T(8,128)(2,1)} async-done(((bf16[1,512,2,128]{3,1,2,0:T(8,128)(2,1)}), bf16[32,512,2,128]{3,1,2,0:T(8,128)(2,1)}) %all-gather.6.cloned.1.call-update) | async-done | bytes 8388624 | tf_op jit(solution)/shard_map/all_gather | solution.py:14
  114.4 4.2 fusion
  118.6 154.2 %all-gather.8.cloned.1.call-done = bf16[4096,2,128]{0,2,1:T(8,128)(2,1)} async-done(((bf16[512,2,128]{0,2,1:T(8,128)(2,1)}), bf16[4096,2,128]{0,2,1:T(8,128)(2,1)}) %all-gather.8.cloned.1.call-update) | async-done | bytes 2097168 | tf_op jit(solution)/shard_map/all_gather | solution.py:72
  272.7 13.2 %fusion.4 = bf16[4096,2,128]{0,2,1:T(8,128)(2,1)} fusion(bf16[2,1,512,4096]{3,2,1,0:T(8,128)(2,1)} %param.11, pred[512,4096]{1,0:T(8,128)(4,1)} %fusion, bf16[4096,2,128]{0,2,1:T(8,128)(2,1)} %all-gather.8.cloned.1.call-done), kind=kOutput, calls=%fused_computation.12 | convolution fusion | flops 2157051904 | bytes 14680064 | tf_op jit(solution)/shard_map/hrn,rhk->nhk/dot_general | solution.py:77
  286.7 1.1 dynamic_update_slice.3
  287.8 78.9 %all-reduce.1 = bf16[2,512,128]{1,2,0:T(8,128)(2,1)S(1)} all-reduce(f32[2,512,128]{1,2,0:T(8,128)S(1)} %dynamic_update_slice.3), channel_id=1, replica_groups=mesh['tm'=32,'space'=8] {'tm','space'}, use_global_device_ids=true, to_apply=%region_3.4 | all-reduce | flops 131072 | bytes 786432 | tf_op jit(solution)/shard_map/psum | solution.py:91
  366.7 2.3 fusion.9
  369.0 2.1 multiply_convert_fusion
  371.8 102.9 %all-gather.10.cloned.1.call-done = bf16[16384,2,128]{0,2,1:T(8,128)(2,1)} async-done(((bf16[512,2,128]{0,2,1:T(8,128)(2,1)}), bf16[16384,2,128]{0,2,1:T(8,128)(2,1)}) %all-gather.10.cloned.1.call-update) | async-done | bytes 8388624 | tf_op jit(solution)/shard_map/all_gather | solution.py:14
  474.7 21.1 %copy.52 = bf16[16384,2,128]{2,1,0:T(2,128)(2,1)} copy(bf16[16384,2,128]{0,2,1:T(8,128)(2,1)} %all-gather.10.cloned.1.call-done) | data formatting | bytes 16777216 | tf_op jit(solution)/shard_map/while | solution.py:29
  495.9 92.2 %while.27 = (s32[]{:T(128)}, f32[512,2,128]{2,1,0:T(2,128)S(1)}, s32[]{:T(128)}, bf16[32,512,2,128]{3,2,1,0:T(2,128)(2,1)}, bf16[32,512,2,1]{2,1,3,0:T(8,128)(2,...) while((s32[]{:T(128)}, f32[512,2,128]{2,1,0:T(2,128)S(1)}, s32[]{:T(128)}, ...), condition=%wide.region_5.6_spmd, body=%wide.region_4.5_spmd.sunk | while | flops 394246 | bytes 1321107 | solution.py:29
  495.9 0.9 bitcast_convert_fusion.5
  496.9 2.0 convert_add_fusion.5
  499.8 2.0 convert_add_fusion.5
  502.8 2.0 convert_add_fusion.5
  505.8 2.0 convert_add_fusion.5
  508.8 2.0 convert_add_fusion.5
  511.7 2.0 convert_add_fusion.5
  514.7 2.0 convert_add_fusion.5
  517.7 2.0 convert_add_fusion.5
  520.7 2.0 convert_add_fusion.5
  523.6 2.0 convert_add_fusion.5
  526.6 2.0 convert_add_fusion.5
  529.6 2.0 convert_add_fusion.5
  532.6 2.0 convert_add_fusion.5
  535.5 2.0 convert_add_fusion.5
  538.5 2.0 convert_add_fusion.5
  541.5 2.0 convert_add_fusion.5
  544.5 2.0 convert_add_fusion.5
  547.4 2.0 convert_add_fusion.5
  550.4 2.0 convert_add_fusion.5
  553.4 2.0 convert_add_fusion.5
  556.3 2.0 convert_add_fusion.5
  559.3 2.0 convert_add_fusion.5
  562.3 2.0 convert_add_fusion.5
  565.3 2.0 convert_add_fusion.5
  568.2 2.0 convert_add_fusion.5
  571.2 2.0 convert_add_fusion.5
  574.2 2.0 convert_add_fusion.5
  577.2 2.0 convert_add_fusion.5
  580.1 2.0 convert_add_fusion.5
  583.1 2.0 convert_add_fusion.5
  586.1 2.0 convert_add_fusion.5
  588.4 1.0 copy.48
  (64 shorter events, 32.1 us)
Async XLA Ops:
  7.2 279.1 %copy-start = (bf16[1,512,2,512]{3,2,1,0:T(2,128)(2,1)S(1)}, bf16[1,512,2,512]{3,2,1,0:T(2,128)(2,1)}, u32[]{:S(2)}) copy-start(bf16[1,512,2,512]{3,2,1,0:T(2,128)(2,1)} %param.15) | copy-start | bytes 3145732
  7.2 105.5 %all-gather.6.cloned.1.call-start = ((), (), s32[]{:S(2)}) async-start(), calls=%async_computation.1 | async-start | bytes 8650752 | tf_op jit(solution)/shard_map/all_gather | solution.py:14
  9.1 263.6 %all-gather.8.cloned.1.call-start = ((), (), s32[]{:S(2)}) async-start(), calls=%async_computation.2 | async-start | bytes 2359296 | tf_op jit(solution)/shard_map/all_gather | solution.py:72
  112.8 0.7 copy-start.2
  112.8 1.6 copy-start.4
  114.3 254.7 %reduce-scatter.2.cloned.1.call-start = ((), (), s32[]{:S(2)}) async-start(), calls=%async_computation.3 | async-start | bytes 2359296 | tf_op jit(solution)/shard_map/reduce_scatter | solution.py:76
  118.6 167.5 %copy-start.3 = (f32[2,2,128]{2,1,0:T(2,128)S(1)}, f32[2,2,128]{2,1,0:T(2,128)}, u32[]{:S(2)}) copy-start(f32[2,2,128]{2,1,0:T(2,128)} %param.16) | copy-start | bytes 6148
  118.6 167.7 %copy-start.1 = (bf16[512,2,128]{0,2,1:T(8,128)(2,1)S(1)}, bf16[512,2,128]{0,2,1:T(8,128)(2,1)}, u32[]{:S(2)}) copy-start(bf16[512,2,128]{0,2,1:T(8,128)(2,1)} %fusion.19) | copy-start | bytes 786436
  286.0 188.7 %all-gather.10.cloned.1.call-start = ((), (), s32[]{:S(2)}) async-start(), calls=%async_computation.4 | async-start | bytes 8650752 | tf_op jit(solution)/shard_map/all_gather | solution.py:14
Sparse Core Ops, SparseCore 0:
  11.2 101.4 all-gather.5
  115.0 157.6 all-gather.7
  286.1 34.6 reduce-scatter.1
  371.3 103.2 all-gather.9
where the time goes:
time: 598 us; the launch traced here: 596 us
  waiting for transfers between devices  303 us (51%)
  blocking collectives  131 us (22%)
  other arithmetic  92.9 us (16%)
  local copies, waits for them, and re-layouts  31.4 us (5%)
  matrix products  22.2 us (4%)
  between operations  14 us (2%)
    all_gather x1, waiting for transfers between devices, on_device(): lax.all_gather(forward_b, 'space', axis=0, tiled=True)  154 us
    all_gather x2, waiting for transfers between devices, carried_in(): lax.all_gather(a.astype(kind), axis)  149 us
    psum x1, blocking collectives, on_device(): fixed_forward = lax.psum(contrib, ('tm', 'space')).astype(jnp.bfloat16)  78.9 us
    add x31, other arithmetic, combine(): value_l + latter[0] * value_e  62.3 us
    all_gather x1, blocking collectives, carried_in(): lax.all_gather(a.astype(kind), axis)  52.1 us
    convert_element_type x31, other arithmetic, one(): lax.dynamic_index_in_dim(a, source, 0, False).astype(own.dtype)  28.8 us
    while x4, local copies, waits for them, and re-layouts, carried_in(): return lax.fori_loop(0, ahead, one, state)  24.8 us
    dot_general x1, matrix products, on_device(): jnp.einsum('hrn,rhk->nhk', block, inner_rows, preferred_element_type=jnp....  13.2 us
  transfers between devices with their start and end apart: 4, of which 3 were waited for; matrix products, arithmetic and copies ran while one was open for 2% of the time, Pallas kernels for 0%

commit v1 on v0

--- a/solution.py
+++ b/solution.py
@@ -88,7 +88,7 @@
     contrib = -coupling
     own_part = lax.dynamic_slice_in_dim(contrib, share_start, share_rows, 1) + fixed_rhs
     contrib = lax.dynamic_update_slice_in_dim(contrib, own_part, share_start, 1)
-    fixed_forward = lax.psum(contrib, ("tm", "space")).astype(jnp.bfloat16)
+    fixed_forward = lax.psum(lax.psum(contrib, "tm"), "space").astype(jnp.bfloat16)
     fixed_total = tip_factor.shape[1]
     fixed_index = jnp.arange(fixed_total, dtype=jnp.int32)
     lower_tri = fixed_index[:, None] >= fixed_index[None, :]

time: 598 us -> 691 us (1.16)
  waiting for transfers between devices: 303 us -> 446 us
  blocking collectives: 131 us -> 79.5 us
    psum x0 -> x1, waiting for transfers between devices: none -> 139 us  [on_device(): lax.psum(contrib, 'tm')]
    psum x1, blocking collectives: 78.9 us -> 27.4 us  [on_device(): lax.psum(lax.psum(contrib, 'tm'), 'space').astype(jnp.bfloat16)]
  transfers between devices with their start and end apart: 4 -> 5, of which waited for: 3 -> 5; matrix products, arithmetic and copies ran while one was open for 2% -> 4% of each run, Pallas kernels for 0% -> 0%
where the time goes in v1:
time: 691 us; the launch traced here: 689 us
  waiting for transfers between devices  446 us (65%)
  other arithmetic  92.9 us (13%)
  blocking collectives  79.5 us (12%)
  local copies, waits for them, and re-layouts  32.3 us (5%)
  matrix products  22.4 us (3%)
  between operations  14 us (2%)
    all_gather x2, waiting for transfers between devices, carried_in(): lax.all_gather(a.astype(kind), axis)  153 us
    all_gather x1, waiting for transfers between devices, on_device(): lax.all_gather(forward_b, 'space', axis=0, tiled=True)  152 us
    psum x1, waiting for transfers between devices, on_device(): lax.psum(contrib, 'tm')  139 us
    add x31, other arithmetic, combine(): value_l + latter[0] * value_e  62.3 us
    all_gather x1, blocking collectives, carried_in(): lax.all_gather(a.astype(kind), axis)  52.1 us
    convert_element_type x31, other arithmetic, one(): lax.dynamic_index_in_dim(a, source, 0, False).astype(own.dtype)  28.8 us
    psum x1, blocking collectives, on_device(): lax.psum(lax.psum(contrib, 'tm'), 'space').astype(jnp.bfloat16)  27.4 us
    while x4, local copies, waits for them, and re-layouts, carried_in(): return lax.fori_loop(0, ahead, one, state)  24.9 us
  transfers between devices with their start and end apart: 5, of which 5 were waited for; matrix products, arithmetic and copies ran while one was open for 4% of the time, Pallas kernels for 0%

profile of v1, /device:TPU:2, one launch (start us, length us, event | category | flops | bytes accessed | tf_op | source)
XLA Modules:
  0.0 688.8 jit_solution(10983389347193668959)
XLA Ops:
  7.2 1.9 copy.62
  9.2 1.2 copy.34
  11.1 52.1 %all-gather = bf16[32,512,2]{1,2,0:T(2,128)(2,1)S(1)} all-gather(bf16[1,512,2]{1,2,0:T(2,128)(2,1)S(1)} %convert_element_type.103), channel_id=2, replica_groups=mesh['tm'=32,'space'=8] {'tm'}, dimensions={0}, use_global_device_ids=true | all-gather | bytes 67584 | tf_op jit(solution)/shard_map/all_gather | solution.py:14
  63.2 3.3 copy.37
  66.6 46.1 %all-gather.6.cloned.1.call-done = bf16[32,512,2,128]{3,1,2,0:T(8,128)(2,1)} async-done(((bf16[1,512,2,128]{3,1,2,0:T(8,128)(2,1)}), bf16[32,512,2,128]{3,1,2,0:T(8,128)(2,1)}) %all-gather.6.cloned.1.call-update) | async-done | bytes 8388624 | tf_op jit(solution)/shard_map/all_gather | solution.py:14
  114.6 4.2 fusion
  119.2 1.1 dynamic_update_slice.3
  121.1 151.6 %all-gather.8.cloned.1.call-done = bf16[4096,2,128]{0,2,1:T(8,128)(2,1)} async-done(((bf16[512,2,128]{0,2,1:T(8,128)(2,1)}), bf16[4096,2,128]{0,2,1:T(8,128)(2,1)}) %all-gather.8.cloned.1.call-update) | async-done | bytes 2097168 | tf_op jit(solution)/shard_map/all_gather | solution.py:72
  272.7 13.4 %fusion.4 = bf16[4096,2,128]{0,2,1:T(8,128)(2,1)} fusion(bf16[2,1,512,4096]{3,2,1,0:T(8,128)(2,1)} %param.11, pred[512,4096]{1,0:T(8,128)(4,1)} %fusion, bf16[4096,2,128]{0,2,1:T(8,128)(2,1)} %all-gather.8.cloned.1.call-done), kind=kOutput, calls=%fused_computation.12 | convolution fusion | flops 2157051904 | bytes 14680064 | tf_op jit(solution)/shard_map/hrn,rhk->nhk/dot_general | solution.py:77
  286.3 139.2 %all-reduce.3.cloned.1.call-done = f32[2,512,128]{1,2,0:T(8,128)} async-done(((f32[2,512,128]{1,2,0:T(8,128)}), f32[2,512,128]{1,2,0:T(8,128)}) %all-reduce.3.cloned.1.call-update) | async-done | bytes 524304 | tf_op jit(solution)/shard_map/psum | solution.py:91
  425.5 27.4 %all-reduce.4 = bf16[2,512,128]{1,2,0:T(8,128)(2,1)S(1)} all-reduce(f32[2,512,128]{1,2,0:T(8,128)} %all-reduce.3.cloned.1.call-done), channel_id=1, replica_groups=mesh['tm'=32,'space'=8] {'space'}, use_global_device_ids=true, to_apply=%region_4.5 | all-reduce | flops 131072 | bytes 786432 | tf_op jit(solution)/shard_map/psum | solution.py:91
  452.9 2.3 fusion.9
  455.3 3.0 reduce-scatter.2.cloned.1.call-done
  458.3 2.1 multiply_convert_fusion
  461.0 106.4 %all-gather.10.cloned.1.call-done = bf16[16384,2,128]{0,2,1:T(8,128)(2,1)} async-done(((bf16[512,2,128]{0,2,1:T(8,128)(2,1)}), bf16[16384,2,128]{0,2,1:T(8,128)(2,1)}) %all-gather.10.cloned.1.call-update) | async-done | bytes 8388624 | tf_op jit(solution)/shard_map/all_gather | solution.py:14
  567.5 21.1 %copy.52 = bf16[16384,2,128]{2,1,0:T(2,128)(2,1)} copy(bf16[16384,2,128]{0,2,1:T(8,128)(2,1)} %all-gather.10.cloned.1.call-done) | data formatting | bytes 16777216 | tf_op jit(solution)/shard_map/while | solution.py:29
  588.7 92.2 %while.27 = (s32[]{:T(128)}, f32[512,2,128]{2,1,0:T(2,128)S(1)}, s32[]{:T(128)}, bf16[32,512,2,128]{3,2,1,0:T(2,128)(2,1)}, bf16[32,512,2,1]{2,1,3,0:T(8,128)(2,...) while((s32[]{:T(128)}, f32[512,2,128]{2,1,0:T(2,128)S(1)}, s32[]{:T(128)}, ...), condition=%wide.region_6.7_spmd, body=%wide.region_5.6_spmd.sunk | while | flops 394246 | bytes 1321107 | solution.py:29
  589.7 2.0 convert_add_fusion.5
  592.7 2.0 convert_add_fusion.5
  595.6 2.0 convert_add_fusion.5
  598.6 2.0 convert_add_fusion.5
  601.6 2.0 convert_add_fusion.5
  604.6 2.0 convert_add_fusion.5
  607.5 2.0 convert_add_fusion.5
  610.5 2.0 convert_add_fusion.5
  613.5 2.0 convert_add_fusion.5
  616.5 2.0 convert_add_fusion.5
  619.4 2.0 convert_add_fusion.5
  622.4 2.0 convert_add_fusion.5
  625.4 2.0 convert_add_fusion.5
  628.4 2.0 convert_add_fusion.5
  631.3 2.0 convert_add_fusion.5
  634.3 2.0 convert_add_fusion.5
  637.3 2.0 convert_add_fusion.5
  640.3 2.0 convert_add_fusion.5
  643.2 2.0 convert_add_fusion.5
  646.2 2.0 convert_add_fusion.5
  649.2 2.0 convert_add_fusion.5
  652.2 2.0 convert_add_fusion.5
  655.1 2.0 convert_add_fusion.5
  658.1 2.0 convert_add_fusion.5
  661.1 2.0 convert_add_fusion.5
  664.1 2.0 convert_add_fusion.5
  667.0 2.0 convert_add_fusion.5
  670.0 2.0 convert_add_fusion.5
  673.0 2.0 convert_add_fusion.5
  676.0 2.0 convert_add_fusion.5
  678.9 2.0 convert_add_fusion.5
  (69 shorter events, 34.8 us)
Async XLA Ops:
  7.2 111.6 %copy-start = (bf16[1,512,2,512]{3,2,1,0:T(2,128)(2,1)S(1)}, bf16[1,512,2,512]{3,2,1,0:T(2,128)(2,1)}, u32[]{:S(2)}) copy-start(bf16[1,512,2,512]{3,2,1,0:T(2,128)(2,1)} %param.15) | copy-start | bytes 3145732
  7.2 105.5 %all-gather.6.cloned.1.call-start = ((), (), s32[]{:S(2)}) async-start(), calls=%async_computation.1 | async-start | bytes 8650752 | tf_op jit(solution)/shard_map/all_gather | solution.py:14
  9.1 263.6 %all-gather.8.cloned.1.call-start = ((), (), s32[]{:S(2)}) async-start(), calls=%async_computation.2 | async-start | bytes 2359296 | tf_op jit(solution)/shard_map/all_gather | solution.py:72
  112.8 0.7 copy-start.3
  112.8 1.6 copy-start.4
  112.8 1.7 copy-start.5
  114.3 311.2 %all-reduce.3.cloned.1.call-start = ((), (), s32[]{:S(2)}) async-start(), calls=%async_computation.4 | async-start | bytes 1048576 | tf_op jit(solution)/shard_map/psum | solution.py:91
  114.5 4.2 copy-start.2
  120.2 0.8 copy-start.1
  121.1 337.2 %reduce-scatter.2.cloned.1.call-start = ((), (), s32[]{:S(2)}) async-start(), calls=%async_computation.3 | async-start | bytes 2359296 | tf_op jit(solution)/shard_map/reduce_scatter | solution.py:76
  286.1 281.3 %all-gather.10.cloned.1.call-start = ((), (), s32[]{:S(2)}) async-start(), calls=%async_computation.5 | async-start | bytes 8650752 | tf_op jit(solution)/shard_map/all_gather | solution.py:14
Sparse Core Ops, SparseCore 0:
  11.2 101.4 all-gather.5
  114.5 158.2 all-gather.7
  276.7 148.7 all-reduce.2
  428.1 30.1 reduce-scatter.1
  461.5 105.9 all-gather.9
